TPU v7x, 32 devices: a whole 2x2x4 slice. The times are simulated.
32 devices in a mesh: dp: 2 (over x), rows: 16 (over z, y, core).
Axes of the slice: x: 2, y: 2, z: 4, core: 2. Of those that a mesh axis runs over, the one named last changes fastest.
Arguments:
- tokens: bfloat16 [16384, 512], P(('dp', 'rows')), may hold values from -6 to 6
- segment_ids: int32 [1024], P(('dp', 'rows')), may hold values from 0 to 169, never falling along the last dimension, each value on 1 to 8 neighbouring positions
- first_gain: float32 [512], replicated, may hold values from 0.1 to 1.9
- first_shift: float32 [512], replicated, may hold values from -4 to 4
- triple_weight: bfloat16 [512, 1536], replicated, may hold values from -0.25 to 0.25
- output_weight: bfloat16 [512, 512], replicated, may hold values from -0.75 to 0.75
- output_bias: float32 [512], replicated, may hold values from -4 to 4
- second_gain: float32 [512], replicated, may hold values from 0.1 to 1.9
- second_shift: float32 [512], replicated, may hold values from -4 to 4
- expand_weight: bfloat16 [512, 2048], replicated, may hold values from -0.25 to 0.25
- expand_bias: float32 [2048], replicated, may hold values from -6 to 6
- reduce_weight: bfloat16 [2048, 512], replicated, may hold values from -0.1875 to 0.1875
- reduce_bias: float32 [512], replicated, may hold values from -4 to 4
- cotangent: bfloat16 [16384, 512], P(('dp', 'rows')), may hold values from -6 to 6
Outputs:
- layer_out: bfloat16 [16384, 512], P(('dp', 'rows'))
- input_grad: bfloat16 [16384, 512], P(('dp', 'rows'))
- grad_first_gain: float32 [512], replicated
- grad_first_shift: float32 [512], replicated
- grad_triple: float32 [512, 1536], replicated
- grad_output: float32 [512, 512], replicated
- grad_output_bias: float32 [512], replicated
- grad_second_gain: float32 [512], replicated
- grad_second_shift: float32 [512], replicated
- grad_expand: float32 [512, 2048], replicated
- grad_expand_bias: float32 [2048], replicated
- grad_reduce: float32 [2048, 512], replicated
- grad_reduce_bias: float32 [512], replicated
Inputs may be any that keep to these rules, and one draw needn't show every extreme that they name: `segment_ids`: sample numbers never fall along the rows and rise by one at each new sample; each sample covers 1 to 8 consecutive rows, and some sample covers exactly 8.
All inputs are finite; a program needn't handle non-finite values.
Results may differ from a plain program's by a relative error of at most 0.011.
Values may be sent and summed in bfloat16 or wider, within the bound.
A program may use at most 128 MiB of HBM per device.

v0:
```python
from functools import partial
import jax
import jax.numpy as jnp
from jax import lax
from jax.sharding import PartitionSpec as P

HEADS = 16
HEAD_DIM = 32
LON = 16
BLOCK_ROWS = 32
EPSILON = 1e-06
NEGATIVE = -1e30


def extended(x, sides, width):
    for axis, dim in sides:
        size, length = (lax.axis_size(axis), x.shape[dim])
        up = [(i, (i + 1) % size) for i in range(size - 1)]
        down = [(j, i) for i, j in up]
        last = lax.slice_in_dim(x, length - width, length, axis=dim)
        initial = lax.slice_in_dim(x, 0, width, axis=dim)
        before = lax.ppermute(last, axis, up)
        after = lax.ppermute(initial, axis, down)
        x = jnp.concatenate([before, x, after], axis=dim)
    return x


def norm_forward(values, norm_gain, norm_shift):
    average = jnp.mean(values, axis=-1, keepdims=True)
    centred = values - average
    inv_dev = lax.rsqrt(jnp.mean(centred * centred, axis=-1, keepdims=True) + EPSILON)
    standard = centred * inv_dev
    return (standard * norm_gain + norm_shift, standard, inv_dev)


def norm_backward(incoming, standard, inv_dev, norm_gain):
    scaled = incoming * norm_gain
    bracket = (
        scaled
        - jnp.mean(scaled, axis=-1, keepdims=True)
        - standard * jnp.mean(scaled * standard, axis=-1, keepdims=True)
    )
    return (inv_dev * bracket, jnp.sum(incoming * standard, axis=0), jnp.sum(incoming, axis=0))


def window_mask(query_seg, key_seg):
    query_row = jnp.repeat(jnp.arange(BLOCK_ROWS, dtype=jnp.int32) + 1, LON)
    key_row = jnp.repeat(jnp.arange(BLOCK_ROWS + 2, dtype=jnp.int32), LON)
    query_lon = jnp.tile(jnp.arange(LON, dtype=jnp.int32), BLOCK_ROWS)
    key_lon = jnp.tile(jnp.arange(LON, dtype=jnp.int32), BLOCK_ROWS + 2)
    lon_gap = (query_lon[:, None] - key_lon[None, :]) % LON
    circle = jnp.minimum(lon_gap, LON - lon_gap)
    nearby = (jnp.abs(query_row[:, None] - key_row[None, :]) <= 1) & (circle <= 2)
    same_sample = jnp.repeat(query_seg, LON)[:, None] == jnp.repeat(key_seg, LON)[None, :]
    return nearby & same_sample


def outer_sum(left, right):
    return lax.dot_general(
        left, right, (((0,), (0,)), ((), ())), preferred_element_type=jnp.float32
    )


def times_transposed(left, right):
    return lax.dot_general(
        left, right, (((1,), (1,)), ((), ())), preferred_element_type=jnp.float32
    )


def head_split(values):
    return values.reshape(values.shape[0], HEADS, HEAD_DIM)


def block_logits(queries, key_rows, allowed):
    scores = jnp.einsum(
        "qhd,khd->hqk",
        head_split(queries),
        head_split(key_rows),
        preferred_element_type=jnp.float32,
    ) * HEAD_DIM ** (-0.5)
    return jnp.where(allowed[None], scores, NEGATIVE)


def total_grads(gradients):
    return lax.psum(gradients, ("dp", "rows"))


def body(
    tokens,
    segment_ids,
    first_gain,
    first_shift,
    triple_weight,
    output_weight,
    output_bias,
    second_gain,
    second_shift,
    expand_weight,
    expand_bias,
    reduce_weight,
    reduce_bias,
    cotangent,
):
    model_width = output_weight.shape[0]
    row_count = segment_ids.shape[0]
    token_count = tokens.shape[0]
    block_count = row_count // BLOCK_ROWS
    query_span = BLOCK_ROWS * LON
    key_span = (BLOCK_ROWS + 2) * LON
    head_scale = HEAD_DIM ** (-0.5)
    inputs = tokens.astype(jnp.float32)
    band_index = lax.axis_index("rows")
    band_count = lax.axis_size("rows")
    seg_ext = extended(segment_ids, (("rows", 0),), 1)
    ext_row = jnp.arange(row_count + 2, dtype=jnp.int32)
    inside = ((ext_row > 0) | (band_index > 0)) & (
        (ext_row < row_count + 1) | (band_index < band_count - 1)
    )
    seg_ext = jnp.where(inside, seg_ext, -1)
    first_out, first_std, first_inv = norm_forward(inputs, first_gain, first_shift)
    first_low = first_out.astype(jnp.bfloat16)
    triple = jnp.dot(first_low, triple_weight, preferred_element_type=jnp.float32).astype(
        jnp.bfloat16
    )
    queries = triple[:, :model_width]
    pair_ext = extended(
        triple[:, model_width:].reshape(row_count, LON, 2 * model_width), (("rows", 0),), 1
    )

    def block_inputs(block_index):
        first_row = block_index * BLOCK_ROWS
        pair_block = pair_ext.reshape(key_span, 2 * model_width)
        allowed = window_mask(
            lax.dynamic_slice_in_dim(seg_ext, first_row + 1, BLOCK_ROWS, 0), seg_ext
        )
        key_rows = pair_block[:, :model_width]
        value_rows = pair_block[:, model_width:]
        return (first_row, queries, key_rows, value_rows, block_logits(queries, key_rows, allowed))

    def forward_block(block_index):
        pieces = block_inputs(block_index)
        logits = pieces[4]
        largest = jnp.max(logits, axis=-1, keepdims=True)
        raised = jnp.exp(logits - largest)
        denominator = jnp.sum(raised, axis=-1, keepdims=True)
        weights = (raised / denominator).astype(jnp.bfloat16)
        mixed = jnp.einsum(
            "hqk,khd->qhd", weights, head_split(pieces[3]), preferred_element_type=jnp.float32
        )
        return (
            mixed.reshape(query_span, model_width).astype(jnp.bfloat16),
            (largest + jnp.log(denominator))[..., 0],
        )

    attended, log_totals = lax.map(forward_block, jnp.arange(block_count, dtype=jnp.int32))
    attended = attended.reshape(token_count, model_width)
    hidden_state = (
        inputs + jnp.dot(attended, output_weight, preferred_element_type=jnp.float32) + output_bias
    )
    second_out, second_std, second_inv = norm_forward(hidden_state, second_gain, second_shift)
    second_low = second_out.astype(jnp.bfloat16)
    expanded = jnp.dot(second_low, expand_weight, preferred_element_type=jnp.float32) + expand_bias
    activated, gelu_back = jax.vjp(partial(jax.nn.gelu, approximate=False), expanded)
    activated_low = activated.astype(jnp.bfloat16)
    layer_out = (
        hidden_state
        + jnp.dot(activated_low, reduce_weight, preferred_element_type=jnp.float32)
        + reduce_bias
    ).astype(jnp.bfloat16)
    upstream = cotangent.astype(jnp.float32)
    grad_reduce = outer_sum(activated_low, cotangent)
    grad_reduce_bias = jnp.sum(upstream, axis=0)
    expanded_grad = gelu_back(times_transposed(cotangent, reduce_weight))[0].astype(jnp.bfloat16)
    grad_expand = outer_sum(second_low, expanded_grad)
    grad_expand_bias = jnp.sum(expanded_grad.astype(jnp.float32), axis=0)
    second_grad = times_transposed(expanded_grad, expand_weight)
    state_part, grad_second_gain, grad_second_shift = norm_backward(
        second_grad, second_std, second_inv, second_gain
    )
    state_grad = upstream + state_part
    feed_totals = total_grads(
        (
            grad_second_gain,
            grad_second_shift,
            grad_expand,
            grad_expand_bias,
            grad_reduce,
            grad_reduce_bias,
        )
    )
    branch_grad = state_grad.astype(jnp.bfloat16)
    grad_output = outer_sum(attended, branch_grad)
    grad_output_bias = jnp.sum(branch_grad.astype(jnp.float32), axis=0)
    attended_grad = times_transposed(branch_grad, output_weight).astype(jnp.bfloat16)

    def backward_block(block_index, state_pair):
        query_grads, pair_grads = state_pair
        first_row, query_block, key_rows, value_rows, logits = block_inputs(block_index)
        weights = jnp.exp(logits - log_totals[block_index][..., None])
        upstream_block = head_split(attended_grad)
        weight_grads = jnp.einsum(
            "qhd,khd->hqk",
            upstream_block,
            head_split(value_rows),
            preferred_element_type=jnp.float32,
        )
        centre = jnp.sum(weights * weight_grads, axis=-1, keepdims=True)
        score_grads = (weights * (weight_grads - centre)).astype(jnp.bfloat16)
        query_part = (
            jnp.einsum(
                "hqk,khd->qhd",
                score_grads,
                head_split(key_rows),
                preferred_element_type=jnp.float32,
            )
            * head_scale
        )
        key_part = (
            jnp.einsum(
                "hqk,qhd->khd",
                score_grads,
                head_split(query_block),
                preferred_element_type=jnp.float32,
            )
            * head_scale
        )
        value_part = jnp.einsum(
            "hqk,qhd->khd",
            weights.astype(jnp.bfloat16),
            upstream_block,
            preferred_element_type=jnp.float32,
        )
        query_grads = query_part.reshape(query_span, model_width)
        pair_part = jnp.concatenate(
            [
                key_part.reshape(BLOCK_ROWS + 2, LON, model_width),
                value_part.reshape(BLOCK_ROWS + 2, LON, model_width),
            ],
            axis=-1,
        )
        current = pair_grads
        pair_grads = current + pair_part
        return (query_grads, pair_grads)

    start_state = (
        jnp.zeros((token_count, model_width), jnp.float32),
        jnp.zeros((row_count + 2, LON, 2 * model_width), jnp.float32),
    )
    query_grads, pair_grads = lax.fori_loop(0, block_count, backward_block, start_state)
    rim_grads = extended(
        jnp.stack([pair_grads[0], pair_grads[row_count + 1]]).astype(jnp.bfloat16),
        (("rows", 0),),
        1,
    ).astype(jnp.float32)
    own_grads = pair_grads[1 : row_count + 1]
    own_grads = own_grads.at[0].add(rim_grads[0]).at[row_count - 1].add(rim_grads[3])
    triple_grad = jnp.concatenate(
        [query_grads, own_grads.reshape(token_count, 2 * model_width)], axis=1
    ).astype(jnp.bfloat16)
    grad_triple = outer_sum(first_low, triple_grad)
    first_grad = times_transposed(triple_grad, triple_weight)
    input_part, grad_first_gain, grad_first_shift = norm_backward(
        first_grad, first_std, first_inv, first_gain
    )
    input_grad = (state_grad + input_part).astype(jnp.bfloat16)
    attention_totals = total_grads(
        (grad_first_gain, grad_first_shift, grad_triple, grad_output, grad_output_bias)
    )
    factor = (token_count * lax.axis_size("dp") * band_count) ** (-0.5)
    return (
        layer_out,
        input_grad,
        attention_totals[0] * factor,
        attention_totals[1] * factor,
        attention_totals[2] * factor,
        attention_totals[3] * factor,
        attention_totals[4] * factor,
        feed_totals[0] * factor,
        feed_totals[1] * factor,
        feed_totals[2] * factor,
        feed_totals[3] * factor,
        feed_totals[4] * factor,
        feed_totals[5] * factor,
    )


def solution(mesh):
    placed = (
        P(("dp", "rows"), None),
        P(("dp", "rows")),
        P(),
        P(),
        P(),
        P(),
        P(),
        P(),
        P(),
        P(),
        P(),
        P(),
        P(),
        P(("dp", "rows"), None),
    )
    return jax.shard_map(
        body,
        mesh=mesh,
        in_specs=placed,
        out_specs=(
            P(("dp", "rows"), None),
            P(("dp", "rows"), None),
            P(),
            P(),
            P(),
            P(),
            P(),
            P(),
            P(),
            P(),
            P(),
            P(),
            P(),
        ),
        check_vma=False,
    )
```

profile of v0, /device:TPU:0, one launch (start us, length us, event | category | flops | bytes accessed | tf_op | source)
XLA Modules:
  0.0 437.1 jit_solution(15989438350053171795)
XLA Ops:
  7.2 1.4 copy.40
  9.0 2.6 convolution_convert_fusion
  12.2 1.4 collective-permute-start.1
  13.6 3.0 collective-permute-start
  17.3 1.3 collective-permute-start.3
  18.5 5.7 %collective-permute-start.2 = (s32[1]{0:T(128)}, s32[1]{0:T(128)}, u32[]{:S(2)}, u32[]{:S(2)}) collective-permute-start(s32[1]{0:T(128)} %get-tuple-element.136), channel_id=1, source_target_pairs={{0,1},{1,2},{2,3},{3,4},{4,5},{5,6},{6,7},{7,8},{8,9},{9,10},{10,1... | collective-permute-start | bytes 20 | tf_op jit(solution)/shard_map/ppermute | solution.py:22
  24.2 1.1 slice.122
  26.2 1.3 copy.42
  28.4 1.0 copy.45
  29.5 1.3 and_select_fusion
  31.2 2.3 fusion.30
  33.5 1.4 pad_maximum_fusion.1
  34.9 0.9 fusion.55
  35.8 1.1 copy.56
  36.9 1.3 copy.57
  38.2 8.4 %fusion.57 = (f32[16,512]{1,0:T(8,128)}, f32[16,512,544]{1,2,0:T(8,128)}) fusion(bf16[512,16,32]{0,2,1:T(8,128)(2,1)S(1)} %bitcast.51, bf16[544,16,32]{0,2,1:T(8,128)(2,1)S(1)} %bitcast.47, pred[512,544]{0,1:T(8,128)(4,1)S(1)} %fusion.30), kind=kOutput, calls=%fused_computation.127 | convolution fusion | flops 298573824 | bytes 19218432 | tf_op jit(solution)/shard_map/while/body/eval_jaxpr/qhd,khd->hqk/dot_general | solution.py:75
  46.7 8.8 %fusion = f32[16,512]{1,0:T(8,128)S(1)} fusion(f32[16,512,544]{1,2,0:T(8,128)} %get-tuple-element.139, f32[16,512]{1,0:T(8,128)} %get-tuple-element.138), kind=kLoop, calls=%fused_computation.6 | loop fusion | flops 8904704 | bytes 17891328 | tf_op jit(solution)/shard_map/while/body/eval_jaxpr/reduce_sum | solution.py:145
  55.6 9.3 %fusion.20 = bf16[16,32,512]{2,1,0:T(8,128)(2,1)S(1)} fusion(bf16[544,16,32]{0,2,1:T(8,128)(2,1)S(1)} %bitcast.56, f32[16,512,544]{1,2,0:T(8,128)} %get-tuple-element.139, f32[16,512]{1,0:T(8,128)S(1)} %fusion, f32[16,512]{1,0:T(8,128)S(1)} %copy-done.31), kind=kOutput, calls=%fused_computation.55 | convolution fusion | flops 298844160 | bytes 18972672 | tf_op jit(solution)/shard_map/while/body/eval_jaxpr/hqk,khd->qhd/dot_general | solution.py:147
  65.7 1.4 fusion.52
  67.1 12.3 %convert_reduce_fusion = (f32[2048]{0:T(1024)S(1)}, bf16[512,2048]{1,0:T(8,128)(2,1)S(1)}, f32[512,2048]{1,0:T(8,128)}) fusion(f32[512,2048]{1,0:T(8,128)S(1)} %fusion.52, f32[2048]{0:T(1024)S(1)} %copy-done.39, bf16[512,512]{1,0:T(8,128)(2,1)S(1)} %copy-done.22, bf16[2048,512]{1,0:T(8,128)(2,1)S(1)} %copy-done), kind=kOutput, calls=%fused_computation.13 | convolution fusion | flops 1152382976 | bytes 13123584 | tf_op jit(solution)/shard_map/dot_general | solution.py:65
  79.5 2.4 fusion.60
  81.9 2.6 copy.46
  84.5 1.7 multiply_reduce_fusion.1
  86.2 2.0 convert_reduce_fusion.3
  88.1 1.0 copy-done.6
  89.6 11.6 %multiply_reduce_fusion = (f32[16,512]{1,0:T(8,128)S(1)}, f32[16,512,544]{1,2,0:T(8,128)}) fusion(f32[16,512,544]{1,2,0:T(8,128)} %get-tuple-element.139, f32[16,512]{1,0:T(8,128)S(1)} %log_add_fusion, bf16[512,16,32]{0,2,1:T(8,128)(2,1)S(1)} %bitcast.49, bf16[544,16,32]{0,2,1:T(8,128)(2,1)S(1)} %bitcast.57), kind=kOutput, calls=%fused_computation.1 | convolution fusion | flops 298573824 | bytes 36798464 | tf_op jit(solution)/shard_map/while/body/eval_jaxpr/qhd,khd->hqk/dot_general | solution.py:201
  101.2 8.6 %fusion.13 = f32[544,16,32]{0,2,1:T(8,128)} fusion(bf16[512,16,32]{0,2,1:T(8,128)(2,1)S(1)} %bitcast.50, f32[16,512,544]{1,2,0:T(8,128)} %get-tuple-element.139, f32[16,512]{1,0:T(8,128)S(1)} %log_add_fusion), kind=kOutput, calls=%fused_computation.45 | convolution fusion | flops 294125568 | bytes 19496960 | tf_op jit(solution)/shard_map/while/body/eval_jaxpr/hqk,qhd->khd/dot_general | solution.py:227
  109.8 12.4 %multiply_convert_fusion = bf16[16,512,544]{1,2,0:T(8,128)(2,1)S(1)} fusion(f32[16,512,544]{1,2,0:T(8,128)} %get-tuple-element.143, f32[16,512,544]{1,2,0:T(8,128)} %get-tuple-element.139, f32[16,512]{1,0:T(8,128)S(1)} %get-tuple-element.142, f32[16,512]{1,0:T(8,128)S(1)} %log_add_fusion), kind=kLoop, calls=%fused_computation | loop fusion | flops 17825792 | bytes 44630016 | tf_op jit(solution)/shard_map/while/body/eval_jaxpr/convert_element_type | solution.py:208
  122.2 3.8 fusion.12
  126.0 2.4 fusion.19
  128.4 3.3 fusion.51
  131.7 2.3 multiply_convert_fusion.1
  134.1 3.9 copy.47
  138.0 4.8 %reshape.436 = f32[34,16,512]{2,1,0:T(8,128)} reshape(f32[544,16,32]{2,1,0:T(8,128)} %copy.47) | data formatting | bytes 2228224 | tf_op jit(solution)/shard_map/while/body/eval_jaxpr/reshape | solution.py:236
  142.7 2.4 constant_dynamic-update-slice_fusion.1
  145.1 3.9 copy.48
  149.0 4.6 %reshape.437 = f32[34,16,512]{2,1,0:T(8,128)} reshape(f32[544,16,32]{2,1,0:T(8,128)} %copy.48) | data formatting | bytes 2228224 | tf_op jit(solution)/shard_map/while/body/eval_jaxpr/reshape | solution.py:237
  153.6 2.5 constant_dynamic-update-slice_fusion
  156.1 1.8 convert.16
  157.9 1.3 collective-permute-start.5
  159.3 4.0 collective-permute-start.4
  163.3 3.3 fusion.61
  166.6 1.4 fusion.46
  168.0 1.5 slice.127
  169.5 2.1 copy.49
  171.6 1.5 fusion.43
  173.1 1.5 fusion.42
  174.5 1.7 convert.17
  176.3 1.0 copy-done.29
  177.3 3.9 fusion.40
  181.9 3.7 fusion.18
  185.6 2.0 copy.53
  187.6 3.9 fusion.59
  191.5 2.6 copy.50
  194.1 1.6 fusion.38
  195.8 2.0 fusion.37
  197.7 1.0 copy.54
  198.7 45.0 %all-reduce = (f32[512]{0:T(512)S(1)}, f32[512]{0:T(512)S(1)}, f32[512]{0:T(512)S(1)}, f32[512]{0:T(512)S(1)}, f32[512]{0:T(512)S(1)}, /*index=5*/f32[2048]{0:T(1024)S(1)}, f32[512]{0:T(512)S(1)}) all-reduce(f32[512]{0:T(512)S(1)} %get-tuple-element.109, ...), channel_id=1, replica_groups=mesh['dp'=2,'rows'=16] {'dp','rows'}, use_global_device_ids=true, to_apply=%region_12.13 | all-reduce | flops 5120 | bytes 40960 | tf_op jit(solution)/shard_map/psum | solution.py:85
  247.8 171.0 %all-reduce.4.cloned.1.call-done = (f32[512,1536]{1,0:T(8,128)}, f32[512,512]{1,0:T(8,128)}, f32[512,2048]{1,0:T(8,128)}, f32[2048,512]{1,0:T(8,128)}) async-done(((f32[512,1536]{1,0:T(8,128)}, f32[512,512]{1,0:T(8,128)}, f32[512,2048]{1,0:T(8,128)}, f32[2048,512]{1,0:T(8,128)}), (f32[512,1536]{1,0:T(8,128)}, f32[512,512]{1,0:T(8,128)}, f32[512,2048]{1,0:T(8,128)}, ...) | async-done | bytes 12582928 | tf_op jit(solution)/shard_map/psum | solution.py:85
  418.7 4.0 broadcast_multiply_fusion.2
  422.7 1.1 broadcast_multiply_fusion.3
  423.8 2.5 broadcast_multiply_fusion.1
  426.2 1.2 copy-done.14
  427.5 2.5 broadcast_multiply_fusion
  (131 shorter events, 9.9 us)
Async XLA Ops:
  7.2 59.9 %copy-start = (bf16[2048,512]{1,0:T(8,128)(2,1)S(1)}, bf16[2048,512]{1,0:T(8,128)(2,1)}, u32[]{:S(2)}) copy-start(bf16[2048,512]{1,0:T(8,128)(2,1)} %param.29) | copy-start | bytes 6291460
  7.2 411.5 %all-reduce.4.cloned.1.call-start = ((), (), s32[]{:S(2)}) async-start(), calls=%async_computation | async-start | bytes 25165824 | tf_op jit(solution)/shard_map/psum | solution.py:85
  8.6 2.9 copy-start.1
  8.8 2.8 copy-start.34
  9.0 7.7 %copy-start.40 = (s32[32]{0:T(128)S(1)}, s32[32]{0:T(128)}, u32[]{:S(2)}) copy-start(s32[32]{0:T(128)} %param.19) | copy-start | bytes 388
  9.0 16.4 %copy-start.36 = (f32[512]{0:T(512)}, f32[512]{0:T(512)S(1)}, u32[]{:S(2)}) copy-start(f32[512]{0:T(512)S(1)} %add_rsqrt_fusion.1) | copy-start | bytes 6148
  12.2 16.2 %copy-start.21 = (bf16[512,512]{1,0:T(8,128)(2,1)S(1)}, bf16[512,512]{1,0:T(8,128)(2,1)}, u32[]{:S(2)}) copy-start(bf16[512,512]{1,0:T(8,128)(2,1)} %param.31) | copy-start | bytes 1572868
  12.2 21.3 %collective-permute-start.1 = (bf16[1,16,1024]{2,1,0:T(8,128)(2,1)}, bf16[1,16,1024]{2,1,0:T(8,128)(2,1)S(1)}, u32[]{:S(2)}, u32[]{:S(2)}) collective-permute-start(bf16[1,16,1024]{2,1,0:T(8,128)(2,1)} %get-tuple-element.130), channel_id=1, source_target_pairs={{1,0},{2,1},{3,2},{4,3},{5,4},{6,5},{7,6},{8,7},{9,8},{10,9},{11,1... | collective-permute-start | bytes 98312 | tf_op jit(solution)/shard_map/ppermute | solution.py:23
  13.6 19.9 %collective-permute-start = (bf16[1,16,1024]{2,1,0:T(8,128)(2,1)S(1)}, bf16[1,16,1024]{2,1,0:T(8,128)(2,1)S(1)}, u32[]{:S(2)}, u32[]{:S(2)}) collective-permute-start(bf16[1,16,1024]{2,1,0:T(8,128)(2,1)S(1)} %get-tuple-element.129), channel_id=1, source_target_pairs={{0,1},{1,2},{2,3},{3,4},{4,5},{5,6},{6,7},{7,8},{8,9},{9,10},{10,1... | collective-permute-start | bytes 98312 | tf_op jit(solution)/shard_map/ppermute | solution.py:22
  17.3 12.2 %collective-permute-start.3 = (s32[1]{0:T(128)}, s32[1]{0:T(128)}, u32[]{:S(2)}, u32[]{:S(2)}) collective-permute-start(s32[1]{0:T(128)} %get-tuple-element.137), channel_id=1, source_target_pairs={{1,0},{2,1},{3,2},{4,3},{5,4},{6,5},{7,6},{8,7},{9,8},{10,9},{11,1... | collective-permute-start | bytes 20 | tf_op jit(solution)/shard_map/ppermute | solution.py:23
  18.5 10.9 %collective-permute-start.2 = (s32[1]{0:T(128)}, s32[1]{0:T(128)}, u32[]{:S(2)}, u32[]{:S(2)}) collective-permute-start(s32[1]{0:T(128)} %get-tuple-element.136), channel_id=1, source_target_pairs={{0,1},{1,2},{2,3},{3,4},{4,5},{5,6},{6,7},{7,8},{8,9},{9,10},{10,1... | collective-permute-start | bytes 20 | tf_op jit(solution)/shard_map/ppermute | solution.py:22
  27.4 10.8 %copy-start.12 = (bf16[512,512]{0,1:T(8,128)(2,1)}, bf16[512,512]{0,1:T(8,128)(2,1)S(1)}, u32[]{:S(2)}) copy-start(bf16[512,512]{0,1:T(8,128)(2,1)S(1)} %copy.42) | copy-start | bytes 1572868
  38.2 8.5 %copy-start.10 = (bf16[544,512]{0,1:T(8,128)(2,1)}, bf16[544,512]{0,1:T(8,128)(2,1)S(1)}, u32[]{:S(2)}) copy-start(bf16[544,512]{0,1:T(8,128)(2,1)S(1)} %copy.57) | copy-start | bytes 1671172
  46.7 8.8 %copy-start.31 = (f32[16,512]{1,0:T(8,128)S(1)}, f32[16,512]{1,0:T(8,128)}, u32[]{:S(2)}) copy-start(f32[16,512]{1,0:T(8,128)} %get-tuple-element.138) | copy-start | bytes 98308
  46.7 8.8 %copy-start.17 = (bf16[544,512]{0,1:T(8,128)(2,1)S(1)}, bf16[544,512]{0,1:T(8,128)(2,1)}, u32[]{:S(2)}) copy-start(bf16[544,512]{0,1:T(8,128)(2,1)} %copy.56) | copy-start | bytes 1671172
  55.5 9.4 %copy-start.2 = (bf16[512,512]{0,1:T(8,128)(2,1)S(1)}, bf16[512,512]{0,1:T(8,128)(2,1)}, u32[]{:S(2)}) copy-start(bf16[512,512]{0,1:T(8,128)(2,1)} %copy-done.1) | copy-start | bytes 1572868
  55.5 9.4 %copy-start.24 = (bf16[512,512]{1,0:T(8,128)(2,1)S(1)}, bf16[512,512]{1,0:T(8,128)(2,1)}, u32[]{:S(2)}) copy-start(bf16[512,512]{1,0:T(8,128)(2,1)} %param.23) | copy-start | bytes 1572868
  55.5 9.4 %copy-start.41 = (f32[512]{0:T(512)S(1)}, f32[512]{0:T(512)}, u32[]{:S(2)}) copy-start(f32[512]{0:T(512)} %param.24) | copy-start | bytes 6148
  55.5 10.1 %copy-start.26 = (bf16[512,2048]{1,0:T(8,128)(2,1)S(1)}, bf16[512,2048]{1,0:T(8,128)(2,1)}, u32[]{:S(2)}) copy-start(bf16[512,2048]{1,0:T(8,128)(2,1)} %param.27) | copy-start | bytes 6291460
  55.5 10.1 %copy-start.32 = (f32[512]{0:T(512)S(1)}, f32[512]{0:T(512)}, u32[]{:S(2)}) copy-start(f32[512]{0:T(512)} %param.25) | copy-start | bytes 6148
  55.6 10.1 %copy-start.33 = (f32[512]{0:T(512)S(1)}, f32[512]{0:T(512)}, u32[]{:S(2)}) copy-start(f32[512]{0:T(512)} %param.26) | copy-start | bytes 6148
  64.9 2.2 copy-start.19
  65.4 1.7 copy-start.22
  65.4 1.7 copy-start.39
  67.1 12.4 %copy-start.4 = (f32[512,2048]{1,0:T(8,128)}, f32[512,2048]{1,0:T(8,128)S(1)}, u32[]{:S(2)}) copy-start(f32[512,2048]{1,0:T(8,128)S(1)} %fusion.52) | copy-start | bytes 12582916
  79.5 2.4 copy-start.27
  84.5 4.7 %copy-start.25 = (bf16[512,512]{1,0:T(8,128)(2,1)S(1)}, bf16[512,512]{1,0:T(8,128)(2,1)}, u32[]{:S(2)}) copy-start(bf16[512,512]{1,0:T(8,128)(2,1)} %param.23) | copy-start | bytes 1572868
  84.5 5.1 %copy-start.18 = (bf16[544,512]{0,1:T(8,128)(2,1)S(1)}, bf16[544,512]{0,1:T(8,128)(2,1)}, u32[]{:S(2)}) copy-start(bf16[544,512]{0,1:T(8,128)(2,1)} %copy.56) | copy-start | bytes 1671172
  88.1 1.0 copy-start.6
  109.8 12.4 %copy-start.13 = (bf16[512,512]{0,1:T(8,128)(2,1)S(1)}, bf16[512,512]{0,1:T(8,128)(2,1)}, u32[]{:S(2)}) copy-start(bf16[512,512]{0,1:T(8,128)(2,1)} %copy-done.12) | copy-start | bytes 1572868
  122.2 3.8 copy-start.11
  126.0 2.4 copy-start.28
  126.0 5.8 %copy-start.16 = (f32[512,2048]{1,0:T(8,128)S(1)}, f32[512,2048]{1,0:T(8,128)}, u32[]{:S(2)}) copy-start(f32[512,2048]{1,0:T(8,128)} %get-tuple-element.126) | copy-start | bytes 12582916
  128.4 3.4 copy-start.5
  153.6 9.6 %copy-start.9 = (bf16[512,2048]{1,0:T(8,128)(2,1)S(1)}, bf16[512,2048]{1,0:T(8,128)(2,1)}, u32[]{:S(2)}) copy-start(bf16[512,2048]{1,0:T(8,128)(2,1)} %multiply_convert_fusion.1) | copy-start | bytes 6291460
  153.6 9.7 %copy-start.23 = (bf16[512,512]{1,0:T(8,128)(2,1)S(1)}, bf16[512,512]{1,0:T(8,128)(2,1)}, u32[]{:S(2)}) copy-start(bf16[512,512]{1,0:T(8,128)(2,1)} %param.31) | copy-start | bytes 1572868
  157.9 13.7 %collective-permute-start.5 = (bf16[1,16,1024]{2,1,0:T(8,128)(2,1)S(1)}, bf16[1,16,1024]{2,1,0:T(8,128)(2,1)S(1)}, u32[]{:S(2)}, u32[]{:S(2)}) collective-permute-start(bf16[1,16,1024]{2,1,0:T(8,128)(2,1)S(1)} %get-tuple-element.132), channel_id=1, source_target_pairs={{1,0},{2,1},{3,2},{4,3},{5,4},{6,5},{7,6},{8,7},{9,8},{10,9},{11,1... | collective-permute-start | bytes 98312 | tf_op jit(solution)/shard_map/ppermute | solution.py:23
  159.2 7.4 %copy-start.7 = (f32[512,512]{0,1:T(8,128)S(1)}, f32[512,512]{0,1:T(8,128)}, u32[]{:S(2)}) copy-start(f32[512,512]{0,1:T(8,128)} %copy-done.6) | copy-start | bytes 3145732
  159.2 7.3 %copy-start.20 = (bf16[16,32,512]{2,1,0:T(8,128)(2,1)S(1)}, bf16[16,32,512]{2,1,0:T(8,128)(2,1)}, u32[]{:S(2)}) copy-start(bf16[16,32,512]{2,1,0:T(8,128)(2,1)} %copy-done.19) | copy-start | bytes 1572868
  159.2 8.8 %copy-start.8 = (f32[34,16,1024]{2,1,0:T(8,128)S(1)}, f32[34,16,1024]{2,1,0:T(8,128)}, u32[]{:S(2)}) copy-start(f32[34,16,1024]{2,1,0:T(8,128)} %constant_dynamic-update-slice_fusion) | copy-start | bytes 6684676
  159.3 12.3 %collective-permute-start.4 = (bf16[1,16,1024]{2,1,0:T(8,128)(2,1)S(1)}, bf16[1,16,1024]{2,1,0:T(8,128)(2,1)S(1)}, u32[]{:S(2)}, u32[]{:S(2)}) collective-permute-start(bf16[1,16,1024]{2,1,0:T(8,128)(2,1)S(1)} %get-tuple-element.131), channel_id=1, source_target_pairs={{0,1},{1,2},{2,3},{3,4},{4,5},{5,6},{6,7},{7,8},{8,9},{9,10},{10,1... | collective-permute-start | bytes 98312 | tf_op jit(solution)/shard_map/ppermute | solution.py:22
  168.0 9.2 %copy-start.35 = (f32[512]{0:T(512)S(1)}, f32[512]{0:T(512)}, u32[]{:S(2)}) copy-start(f32[512]{0:T(512)} %copy-done.34) | copy-start | bytes 6148
  168.0 9.2 %copy-start.37 = (f32[512]{0:T(512)S(1)}, f32[512]{0:T(512)}, u32[]{:S(2)}) copy-start(f32[512]{0:T(512)} %copy-done.36) | copy-start | bytes 6148
  168.0 9.2 %copy-start.38 = (f32[512]{0:T(512)S(1)}, f32[512]{0:T(512)}, u32[]{:S(2)}) copy-start(f32[512]{0:T(512)} %param.20) | copy-start | bytes 6148
  168.0 9.2 %copy-start.42 = (f32[512]{0:T(512)S(1)}, f32[512]{0:T(512)}, u32[]{:S(2)}) copy-start(f32[512]{0:T(512)} %param.21) | copy-start | bytes 6148
  176.3 1.0 copy-start.29
  181.2 0.7 copy-start.43
  187.6 6.5 %copy-start.3 = (bf16[512,512]{0,1:T(8,128)(2,1)S(1)}, bf16[512,512]{0,1:T(8,128)(2,1)}, u32[]{:S(2)}) copy-start(bf16[512,512]{0,1:T(8,128)(2,1)} %copy-done.1) | copy-start | bytes 1572868
  418.7 4.0 copy-start.30
  418.7 5.0 %copy-start.15 = (f32[512,2048]{1,0:T(8,128)S(1)}, f32[512,2048]{1,0:T(8,128)}, u32[]{:S(2)}) copy-start(f32[512,2048]{1,0:T(8,128)} %get-tuple-element.122) | copy-start | bytes 12582916
  423.8 3.7 copy-start.14
Sparse Core Ops, SparseCore 0:
  181.3 237.3 all-reduce.3
where the time goes:
time: 441 us; the launch traced here: 437 us
  waiting for transfers between devices  171 us (39%)
  matrix products  83.4 us (19%)
  other arithmetic  56.8 us (13%)
  local copies, waits for them, and re-layouts  49.3 us (11%)
  blocking collectives  45 us (10%)
  starting transfers between devices  16.7 us (4%)
  between operations  14.9 us (3%)
    psum x1, waiting for transfers between devices, total_grads(): return lax.psum(gradients, ('dp', 'rows'))  171 us
    psum x1, blocking collectives, total_grads(): return lax.psum(gradients, ('dp', 'rows'))  45 us
    dot_general x4, matrix products, times_transposed(): lax.dot_general(left, right, (((1,), (1,)), ((), ())), preferred_element_...  19.1 us
    unnamed x95, local copies, waits for them, and re-layouts  14.3 us
    ppermute x3, starting transfers between devices, extended(): before = lax.ppermute(last, axis, up)  12.7 us
    convert_element_type x1, other arithmetic, backward_block(): score_grads = (weights * (weight_grads - centre)).astype(jnp.bfloat16)  12.4 us
    dot_general x4, matrix products, outer_sum(): lax.dot_general(left, right, (((0,), (0,)), ((), ())), preferred_element_...  12 us
    dot_general x1, matrix products, backward_block(): jnp.einsum('qhd,khd->hqk', upstream_block, head_split(value_rows), prefer...  11.6 us
  transfers between devices with their start and end apart: 7, of which 1 were waited for; matrix products, arithmetic and copies ran while one was open for 9% of the time, Pallas kernels for 0%

commit v1 on v0

--- a/solution.py
+++ b/solution.py
@@ -82,7 +82,7 @@
 
 
 def total_grads(gradients):
-    return lax.psum(gradients, ("dp", "rows"))
+    return lax.psum(lax.psum(gradients, "rows"), "dp")
 
 
 def body(

time: 441 us -> 736 us (1.67)
  waiting for transfers between devices: 171 us -> 442 us
  blocking collectives: 45 us -> 68.3 us
    psum x1 -> x2, waiting for transfers between devices: 171 us -> 442 us  [total_grads(): return lax.psum(lax.psum(gradients, 'rows'), 'dp')]
    psum x1 -> x2, blocking collectives: 45 us -> 68.3 us  [total_grads(): return lax.psum(lax.psum(gradients, 'rows'), 'dp')]
  transfers between devices with their start and end apart: 7 -> 8, of which waited for: 1 -> 2; matrix products, arithmetic and copies ran while one was open for 9% -> 5% of each run, Pallas kernels for 0% -> 0%
where the time goes in v1:
time: 736 us; the launch traced here: 732 us
  waiting for transfers between devices  442 us (60%)
  matrix products  83.9 us (11%)
  blocking collectives  68.3 us (9%)
  other arithmetic  56.8 us (8%)
  local copies, waits for them, and re-layouts  49.3 us (7%)
  starting transfers between devices  16.8 us (2%)
  between operations  14.9 us (2%)
    psum x2, waiting for transfers between devices, total_grads(): return lax.psum(lax.psum(gradients, 'rows'), 'dp')  442 us
    psum x2, blocking collectives, total_grads(): return lax.psum(lax.psum(gradients, 'rows'), 'dp')  68.3 us
    dot_general x4, matrix products, times_transposed(): lax.dot_general(left, right, (((1,), (1,)), ((), ())), preferred_element_...  19.5 us
  transfers between devices with their start and end apart: 8, of which 2 were waited for; matrix products, arithmetic and copies ran while one was open for 5% of the time, Pallas kernels for 0%

profile of v1, /device:TPU:0, one launch (start us, length us, event | category | flops | bytes accessed | tf_op | source)
XLA Modules:
  0.0 732.0 jit_solution(12338281209251313401)
XLA Ops:
  7.2 1.4 copy.40
  9.0 2.6 convolution_convert_fusion
  12.2 1.4 collective-permute-start.1
  13.6 3.0 collective-permute-start
  17.3 1.3 collective-permute-start.3
  18.5 5.7 collective-permute-start.2
  24.2 1.1 slice.122
  26.2 1.3 copy.42
  28.4 1.0 copy.45
  29.5 1.3 and_select_fusion
  31.2 2.3 fusion.30
  33.5 1.4 pad_maximum_fusion.1
  35.8 1.1 copy.56
  36.9 1.3 copy.57
  38.2 8.4 %fusion.57 = (f32[16,512]{1,0:T(8,128)}, f32[16,512,544]{1,2,0:T(8,128)}) fusion(bf16[512,16,32]{0,2,1:T(8,128)(2,1)S(1)} %bitcast.51, bf16[544,16,32]{0,2,1:T(8,128)(2,1)S(1)} %bitcast.47, pred[512,544]{0,1:T(8,128)(4,1)S(1)} %fusion.30), kind=kOutput, calls=%fused_computation.127 | convolution fusion | flops 298573824 | bytes 19218432 | tf_op jit(solution)/shard_map/while/body/eval_jaxpr/qhd,khd->hqk/dot_general | solution.py:75
  46.7 8.8 %fusion = f32[16,512]{1,0:T(8,128)S(1)} fusion(f32[16,512,544]{1,2,0:T(8,128)} %get-tuple-element.150, f32[16,512]{1,0:T(8,128)} %get-tuple-element.149), kind=kLoop, calls=%fused_computation.6 | loop fusion | flops 8904704 | bytes 17891328 | tf_op jit(solution)/shard_map/while/body/eval_jaxpr/reduce_sum | solution.py:145
  55.6 9.3 %fusion.20 = bf16[16,32,512]{2,1,0:T(8,128)(2,1)S(1)} fusion(bf16[544,16,32]{0,2,1:T(8,128)(2,1)S(1)} %bitcast.56, f32[16,512,544]{1,2,0:T(8,128)} %get-tuple-element.150, f32[16,512]{1,0:T(8,128)S(1)} %fusion, f32[16,512]{1,0:T(8,128)S(1)} %copy-done.31), kind=kOutput, calls=%fused_computation.55 | convolution fusion | flops 298844160 | bytes 18972672 | tf_op jit(solution)/shard_map/while/body/eval_jaxpr/hqk,khd->qhd/dot_general | solution.py:147
  65.7 1.4 fusion.52
  67.1 12.3 %convert_reduce_fusion = (f32[2048]{0:T(1024)S(1)}, bf16[512,2048]{1,0:T(8,128)(2,1)S(1)}, f32[512,2048]{1,0:T(8,128)}) fusion(f32[512,2048]{1,0:T(8,128)S(1)} %fusion.52, f32[2048]{0:T(1024)S(1)} %copy-done.39, bf16[512,512]{1,0:T(8,128)(2,1)S(1)} %copy-done.22, bf16[2048,512]{1,0:T(8,128)(2,1)S(1)} %copy-done), kind=kOutput, calls=%fused_computation.13 | convolution fusion | flops 1152382976 | bytes 13123584 | tf_op jit(solution)/shard_map/dot_general | solution.py:65
  79.5 2.4 fusion.60
  81.9 2.6 copy.46
  84.5 1.7 multiply_reduce_fusion.1
  86.2 2.0 convert_reduce_fusion.3
  89.6 11.6 %multiply_reduce_fusion = (f32[16,512]{1,0:T(8,128)S(1)}, f32[16,512,544]{1,2,0:T(8,128)}) fusion(f32[16,512,544]{1,2,0:T(8,128)} %get-tuple-element.150, f32[16,512]{1,0:T(8,128)S(1)} %log_add_fusion, bf16[512,16,32]{0,2,1:T(8,128)(2,1)S(1)} %bitcast.49, bf16[544,16,32]{0,2,1:T(8,128)(2,1)S(1)} %bitcast.57), kind=kOutput, calls=%fused_computation.1 | convolution fusion | flops 298573824 | bytes 36798464 | tf_op jit(solution)/shard_map/while/body/eval_jaxpr/qhd,khd->hqk/dot_general | solution.py:201
  101.2 8.6 %fusion.13 = f32[544,16,32]{0,2,1:T(8,128)} fusion(bf16[512,16,32]{0,2,1:T(8,128)(2,1)S(1)} %bitcast.50, f32[16,512,544]{1,2,0:T(8,128)} %get-tuple-element.150, f32[16,512]{1,0:T(8,128)S(1)} %log_add_fusion), kind=kOutput, calls=%fused_computation.45 | convolution fusion | flops 294125568 | bytes 19496960 | tf_op jit(solution)/shard_map/while/body/eval_jaxpr/hqk,qhd->khd/dot_general | solution.py:227
  109.8 12.4 %multiply_convert_fusion = bf16[16,512,544]{1,2,0:T(8,128)(2,1)S(1)} fusion(f32[16,512,544]{1,2,0:T(8,128)} %get-tuple-element.154, f32[16,512,544]{1,2,0:T(8,128)} %get-tuple-element.150, f32[16,512]{1,0:T(8,128)S(1)} %get-tuple-element.153, f32[16,512]{1,0:T(8,128)S(1)} %log_add_fusion), kind=kLoop, calls=%fused_computation | loop fusion | flops 17825792 | bytes 44630016 | tf_op jit(solution)/shard_map/while/body/eval_jaxpr/convert_element_type | solution.py:208
  122.2 3.8 fusion.12
  126.0 2.4 fusion.19
  128.4 3.3 fusion.51
  131.7 2.3 multiply_convert_fusion.1
  134.1 3.9 copy.47
  138.0 4.8 reshape.436
  142.7 2.4 constant_dynamic-update-slice_fusion.1
  145.1 3.9 copy.48
  149.0 4.6 reshape.437
  153.6 2.5 constant_dynamic-update-slice_fusion
  156.1 1.8 convert.16
  157.9 1.3 collective-permute-start.5
  159.3 4.0 collective-permute-start.4
  163.3 3.3 fusion.61
  166.6 1.5 fusion.46
  168.1 1.5 slice.127
  169.6 2.0 copy.49
  171.6 1.5 fusion.43
  173.1 1.5 fusion.42
  174.6 1.7 convert.17
  176.3 1.1 copy-done.29
  177.4 3.9 fusion.40
  181.4 238.9 %all-reduce.7.cloned.1.call-done = (f32[512,1536]{1,0:T(8,128)}, f32[512,512]{1,0:T(8,128)}, f32[512,2048]{1,0:T(8,128)}, f32[2048,512]{1,0:T(8,128)}) async-done(((f32[512,1536]{1,0:T(8,128)}, f32[512,512]{1,0:T(8,128)}, f32[512,2048]{1,0:T(8,128)}, f32[2048,512]{1,0:T(8,128)}), (f32[512,1536]{1,0:T(8,128)}, f32[512,512]{1,0:T(8,128)}, f32[512,2048]{1,0:T(8,128)}, ...) | async-done | bytes 12582928 | tf_op jit(solution)/shard_map/psum | solution.py:85
  421.0 3.7 fusion.18
  424.7 2.0 copy.53
  426.8 4.3 fusion.59
  431.1 2.5 copy.50
  433.6 1.6 fusion.38
  435.3 1.9 fusion.37
  437.2 1.0 copy.54
  438.2 59.5 %all-reduce = (f32[512]{0:T(512)S(1)}, f32[512]{0:T(512)S(1)}, f32[512]{0:T(512)S(1)}, f32[512]{0:T(512)S(1)}, f32[512]{0:T(512)S(1)}, /*index=5*/f32[2048]{0:T(1024)S(1)}, f32[512]{0:T(512)S(1)}) all-reduce(f32[512]{0:T(512)S(1)} %get-tuple-element.109, f32[512]{0:T(512)S(1)} %get-tuple-element.155, ...), channel_id=1, replica_groups=mesh['dp'=2,'rows'=16] {'rows'}, use_global_device_ids=true, to_apply=%region_12.13 | all-reduce | flops 5120 | bytes 40960 | tf_op jit(solution)/shard_map/psum | solution.py:85
  497.7 8.7 %all-reduce.2 = (f32[512]{0:T(512)S(1)}, f32[512]{0:T(512)S(1)}, f32[512]{0:T(512)S(1)}, f32[512]{0:T(512)S(1)}, f32[512]{0:T(512)S(1)}, /*index=5*/f32[2048]{0:T(1024)S(1)}, f32[512]{0:T(512)S(1)}) all-reduce(f32[512]{0:T(512)S(1)} %get-tuple-element.113, f32[512]{0:T(512)S(1)} %get-tuple-element.114, ...), channel_id=1, replica_groups=mesh['dp'=2,'rows'=16] {'dp'}, use_global_device_ids=true, to_apply=%region_13.14 | all-reduce | flops 5120 | bytes 40960 | tf_op jit(solution)/shard_map/psum | solution.py:85
  510.5 203.1 %all-reduce.9.cloned.1.call-done = (f32[512,1536]{1,0:T(8,128)}, f32[512,512]{1,0:T(8,128)}, f32[512,2048]{1,0:T(8,128)}, f32[2048,512]{1,0:T(8,128)}) async-done(((f32[512,1536]{1,0:T(8,128)}, f32[512,512]{1,0:T(8,128)}, f32[512,2048]{1,0:T(8,128)}, f32[2048,512]{1,0:T(8,128)}), (f32[512,1536]{1,0:T(8,128)}, f32[512,512]{1,0:T(8,128)}, f32[512,2048]{1,0:T(8,128)}, ...) | async-done | bytes 12582928 | tf_op jit(solution)/shard_map/psum | solution.py:85
  713.7 4.0 broadcast_multiply_fusion.2
  717.6 1.1 broadcast_multiply_fusion.3
  718.7 2.5 broadcast_multiply_fusion.1
  721.2 1.2 copy-done.14
  722.4 2.5 broadcast_multiply_fusion
  (135 shorter events, 11.8 us)
Async XLA Ops:
  7.2 59.9 %copy-start = (bf16[2048,512]{1,0:T(8,128)(2,1)S(1)}, bf16[2048,512]{1,0:T(8,128)(2,1)}, u32[]{:S(2)}) copy-start(bf16[2048,512]{1,0:T(8,128)(2,1)} %param.29) | copy-start | bytes 6291460
  7.2 413.2 %all-reduce.7.cloned.1.call-start = ((), (), s32[]{:S(2)}) async-start(), calls=%async_computation | async-start | bytes 25165824 | tf_op jit(solution)/shard_map/psum | solution.py:85
  8.6 2.9 copy-start.1
  8.8 2.8 copy-start.34
  9.0 7.7 %copy-start.40 = (s32[32]{0:T(128)S(1)}, s32[32]{0:T(128)}, u32[]{:S(2)}) copy-start(s32[32]{0:T(128)} %param.19) | copy-start | bytes 388
  9.0 16.4 %copy-start.36 = (f32[512]{0:T(512)}, f32[512]{0:T(512)S(1)}, u32[]{:S(2)}) copy-start(f32[512]{0:T(512)S(1)} %add_rsqrt_fusion.1) | copy-start | bytes 6148
  12.2 16.2 %copy-start.21 = (bf16[512,512]{1,0:T(8,128)(2,1)S(1)}, bf16[512,512]{1,0:T(8,128)(2,1)}, u32[]{:S(2)}) copy-start(bf16[512,512]{1,0:T(8,128)(2,1)} %param.31) | copy-start | bytes 1572868
  12.2 21.3 %collective-permute-start.1 = (bf16[1,16,1024]{2,1,0:T(8,128)(2,1)}, bf16[1,16,1024]{2,1,0:T(8,128)(2,1)S(1)}, u32[]{:S(2)}, u32[]{:S(2)}) collective-permute-start(bf16[1,16,1024]{2,1,0:T(8,128)(2,1)} %get-tuple-element.141), channel_id=1, source_target_pairs={{1,0},{2,1},{3,2},{4,3},{5,4},{6,5},{7,6},{8,7},{9,8},{10,9},{11,1... | collective-permute-start | bytes 98312 | tf_op jit(solution)/shard_map/ppermute | solution.py:23
  13.6 19.9 %collective-permute-start = (bf16[1,16,1024]{2,1,0:T(8,128)(2,1)S(1)}, bf16[1,16,1024]{2,1,0:T(8,128)(2,1)S(1)}, u32[]{:S(2)}, u32[]{:S(2)}) collective-permute-start(bf16[1,16,1024]{2,1,0:T(8,128)(2,1)S(1)} %get-tuple-element.140), channel_id=1, source_target_pairs={{0,1},{1,2},{2,3},{3,4},{4,5},{5,6},{6,7},{7,8},{8,9},{9,10},{10,1... | collective-permute-start | bytes 98312 | tf_op jit(solution)/shard_map/ppermute | solution.py:22
  17.3 12.2 %collective-permute-start.3 = (s32[1]{0:T(128)}, s32[1]{0:T(128)}, u32[]{:S(2)}, u32[]{:S(2)}) collective-permute-start(s32[1]{0:T(128)} %get-tuple-element.148), channel_id=1, source_target_pairs={{1,0},{2,1},{3,2},{4,3},{5,4},{6,5},{7,6},{8,7},{9,8},{10,9},{11,1... | collective-permute-start | bytes 20 | tf_op jit(solution)/shard_map/ppermute | solution.py:23
  18.5 10.9 %collective-permute-start.2 = (s32[1]{0:T(128)}, s32[1]{0:T(128)}, u32[]{:S(2)}, u32[]{:S(2)}) collective-permute-start(s32[1]{0:T(128)} %get-tuple-element.147), channel_id=1, source_target_pairs={{0,1},{1,2},{2,3},{3,4},{4,5},{5,6},{6,7},{7,8},{8,9},{9,10},{10,1... | collective-permute-start | bytes 20 | tf_op jit(solution)/shard_map/ppermute | solution.py:22
  27.4 10.8 %copy-start.12 = (bf16[512,512]{0,1:T(8,128)(2,1)}, bf16[512,512]{0,1:T(8,128)(2,1)S(1)}, u32[]{:S(2)}) copy-start(bf16[512,512]{0,1:T(8,128)(2,1)S(1)} %copy.42) | copy-start | bytes 1572868
  38.2 8.5 %copy-start.10 = (bf16[544,512]{0,1:T(8,128)(2,1)}, bf16[544,512]{0,1:T(8,128)(2,1)S(1)}, u32[]{:S(2)}) copy-start(bf16[544,512]{0,1:T(8,128)(2,1)S(1)} %copy.57) | copy-start | bytes 1671172
  46.7 8.8 %copy-start.31 = (f32[16,512]{1,0:T(8,128)S(1)}, f32[16,512]{1,0:T(8,128)}, u32[]{:S(2)}) copy-start(f32[16,512]{1,0:T(8,128)} %get-tuple-element.149) | copy-start | bytes 98308
  46.7 8.8 %copy-start.17 = (bf16[544,512]{0,1:T(8,128)(2,1)S(1)}, bf16[544,512]{0,1:T(8,128)(2,1)}, u32[]{:S(2)}) copy-start(bf16[544,512]{0,1:T(8,128)(2,1)} %copy.56) | copy-start | bytes 1671172
  55.5 9.4 %copy-start.2 = (bf16[512,512]{0,1:T(8,128)(2,1)S(1)}, bf16[512,512]{0,1:T(8,128)(2,1)}, u32[]{:S(2)}) copy-start(bf16[512,512]{0,1:T(8,128)(2,1)} %copy-done.1) | copy-start | bytes 1572868
  55.5 9.4 %copy-start.24 = (bf16[512,512]{1,0:T(8,128)(2,1)S(1)}, bf16[512,512]{1,0:T(8,128)(2,1)}, u32[]{:S(2)}) copy-start(bf16[512,512]{1,0:T(8,128)(2,1)} %param.23) | copy-start | bytes 1572868
  55.5 9.4 %copy-start.41 = (f32[512]{0:T(512)S(1)}, f32[512]{0:T(512)}, u32[]{:S(2)}) copy-start(f32[512]{0:T(512)} %param.24) | copy-start | bytes 6148
  55.5 10.1 %copy-start.26 = (bf16[512,2048]{1,0:T(8,128)(2,1)S(1)}, bf16[512,2048]{1,0:T(8,128)(2,1)}, u32[]{:S(2)}) copy-start(bf16[512,2048]{1,0:T(8,128)(2,1)} %param.27) | copy-start | bytes 6291460
  55.5 10.1 %copy-start.32 = (f32[512]{0:T(512)S(1)}, f32[512]{0:T(512)}, u32[]{:S(2)}) copy-start(f32[512]{0:T(512)} %param.25) | copy-start | bytes 6148
  55.6 10.1 %copy-start.33 = (f32[512]{0:T(512)S(1)}, f32[512]{0:T(512)}, u32[]{:S(2)}) copy-start(f32[512]{0:T(512)} %param.26) | copy-start | bytes 6148
  64.9 2.2 copy-start.19
  65.4 1.7 copy-start.22
  65.4 1.7 copy-start.39
  67.1 12.4 %copy-start.4 = (f32[512,2048]{1,0:T(8,128)}, f32[512,2048]{1,0:T(8,128)S(1)}, u32[]{:S(2)}) copy-start(f32[512,2048]{1,0:T(8,128)S(1)} %fusion.52) | copy-start | bytes 12582916
  79.5 2.4 copy-start.27
  84.5 4.7 copy-start.25
  84.5 5.1 copy-start.18
  88.1 1.0 copy-start.6
  109.8 12.4 %copy-start.13 = (bf16[512,512]{0,1:T(8,128)(2,1)S(1)}, bf16[512,512]{0,1:T(8,128)(2,1)}, u32[]{:S(2)}) copy-start(bf16[512,512]{0,1:T(8,128)(2,1)} %copy-done.12) | copy-start | bytes 1572868
  122.2 3.8 copy-start.11
  126.0 2.4 copy-start.28
  126.0 5.8 copy-start.16
  128.4 3.4 copy-start.5
  153.6 9.6 %copy-start.9 = (bf16[512,2048]{1,0:T(8,128)(2,1)S(1)}, bf16[512,2048]{1,0:T(8,128)(2,1)}, u32[]{:S(2)}) copy-start(bf16[512,2048]{1,0:T(8,128)(2,1)} %multiply_convert_fusion.1) | copy-start | bytes 6291460
  153.6 9.7 %copy-start.23 = (bf16[512,512]{1,0:T(8,128)(2,1)S(1)}, bf16[512,512]{1,0:T(8,128)(2,1)}, u32[]{:S(2)}) copy-start(bf16[512,512]{1,0:T(8,128)(2,1)} %param.31) | copy-start | bytes 1572868
  157.9 13.7 %collective-permute-start.5 = (bf16[1,16,1024]{2,1,0:T(8,128)(2,1)S(1)}, bf16[1,16,1024]{2,1,0:T(8,128)(2,1)S(1)}, u32[]{:S(2)}, u32[]{:S(2)}) collective-permute-start(bf16[1,16,1024]{2,1,0:T(8,128)(2,1)S(1)} %get-tuple-element.143), channel_id=1, source_target_pairs={{1,0},{2,1},{3,2},{4,3},{5,4},{6,5},{7,6},{8,7},{9,8},{10,9},{11,1... | collective-permute-start | bytes 98312 | tf_op jit(solution)/shard_map/ppermute | solution.py:23
  159.2 7.4 %copy-start.7 = (f32[512,512]{0,1:T(8,128)S(1)}, f32[512,512]{0,1:T(8,128)}, u32[]{:S(2)}) copy-start(f32[512,512]{0,1:T(8,128)} %copy-done.6) | copy-start | bytes 3145732
  159.2 7.3 %copy-start.20 = (bf16[16,32,512]{2,1,0:T(8,128)(2,1)S(1)}, bf16[16,32,512]{2,1,0:T(8,128)(2,1)}, u32[]{:S(2)}) copy-start(bf16[16,32,512]{2,1,0:T(8,128)(2,1)} %copy-done.19) | copy-start | bytes 1572868
  159.2 8.8 %copy-start.8 = (f32[34,16,1024]{2,1,0:T(8,128)S(1)}, f32[34,16,1024]{2,1,0:T(8,128)}, u32[]{:S(2)}) copy-start(f32[34,16,1024]{2,1,0:T(8,128)} %constant_dynamic-update-slice_fusion) | copy-start | bytes 6684676
  159.3 12.4 %collective-permute-start.4 = (bf16[1,16,1024]{2,1,0:T(8,128)(2,1)S(1)}, bf16[1,16,1024]{2,1,0:T(8,128)(2,1)S(1)}, u32[]{:S(2)}, u32[]{:S(2)}) collective-permute-start(bf16[1,16,1024]{2,1,0:T(8,128)(2,1)S(1)} %get-tuple-element.142), channel_id=1, source_target_pairs={{0,1},{1,2},{2,3},{3,4},{4,5},{5,6},{6,7},{7,8},{8,9},{9,10},{10,1... | collective-permute-start | bytes 98312 | tf_op jit(solution)/shard_map/ppermute | solution.py:22
  168.1 9.3 %copy-start.35 = (f32[512]{0:T(512)S(1)}, f32[512]{0:T(512)}, u32[]{:S(2)}) copy-start(f32[512]{0:T(512)} %copy-done.34) | copy-start | bytes 6148
  168.1 9.3 %copy-start.37 = (f32[512]{0:T(512)S(1)}, f32[512]{0:T(512)}, u32[]{:S(2)}) copy-start(f32[512]{0:T(512)} %copy-done.36) | copy-start | bytes 6148
  168.1 9.3 %copy-start.38 = (f32[512]{0:T(512)S(1)}, f32[512]{0:T(512)}, u32[]{:S(2)}) copy-start(f32[512]{0:T(512)} %param.20) | copy-start | bytes 6148
  168.1 9.3 %copy-start.42 = (f32[512]{0:T(512)S(1)}, f32[512]{0:T(512)}, u32[]{:S(2)}) copy-start(f32[512]{0:T(512)} %param.21) | copy-start | bytes 6148
  176.3 1.1 copy-start.29
  181.4 532.3 %all-reduce.9.cloned.1.call-start = ((), (), s32[]{:S(2)}) async-start(), calls=%async_computation.1 | async-start | bytes 25165824 | tf_op jit(solution)/shard_map/psum | solution.py:85
  420.4 0.7 copy-start.43
  426.8 6.9 copy-start.3
  713.7 4.0 copy-start.30
  713.7 5.0 copy-start.15
  718.7 3.7 copy-start.14
Sparse Core Ops, SparseCore 0:
  181.5 238.8 all-reduce.6
  423.0 290.6 all-reduce.8
